TPU v7x, 32 devices: a whole 2x2x4 slice. The times are simulated.
32 devices in a mesh: dp: 4 (over z), expert: 4 (over y, x), tensor: 2 (over core).
Axes of the slice: x: 2, y: 2, z: 4, core: 2. Of those that a mesh axis runs over, the one named last changes fastest.
Arguments:
- tokens: bfloat16 [512, 6144], P('dp'), may hold values from -6 to 6
- norm_gain: float32 [6144], replicated, may hold values from 0.1 to 1.9
- expert_ids: int32 [512, 2], P('dp'), may hold values from 0 to 3, all different within a row; in each aligned block of 128 rows (0 to 127, 128 to 255, ...) at most 72 rows name the same one
- gate_weights: float32 [512, 2], P('dp'), may hold values from 0.1 to 0.9
- w_gate: bfloat16 [4, 6144, 12288], P('expert', None, ('dp', 'tensor')), may hold values from -0.078125 to 0.078125
- w_up: bfloat16 [4, 6144, 12288], P('expert', None, ('dp', 'tensor')), may hold values from -0.078125 to 0.078125
- w_down: bfloat16 [4, 12288, 6144], P('expert', 'dp', 'tensor'), may hold values from -0.0546875 to 0.0546875
- label_rows: bfloat16 [512, 6144], P(('dp', 'expert'), 'tensor'), may hold values from -4 to 4, as said below
- seg_ids: int32 [4, 128], P('dp'), may hold values from 0 to 3, never falling along the last dimension, each value on 1 to 64 neighbouring positions
- pair_slot: int32 [4, 4], P('dp'), may hold values from 0 to 3, each once within a row
- ref_scores: float32 [4, 4], P('dp'), may hold values from -8 to 8
Outputs:
- layer_out: bfloat16 [512, 6144], P(('dp', 'expert'), 'tensor')
- margins: float32 [4, 2], P('dp')
Inputs may be any that keep to these rules, and one draw needn't show every extreme that they name: `expert_ids`: each row names two different experts. Among the 128 rows of one dp group no expert is named more than 72 times, and in some group some expert is named exactly 72 times. `seg_ids`: within each row sequence numbers never fall; every sequence has 1 to 64 tokens and one has exactly 64. `pair_slot`: each row holds every number of 0 to 3 once. `label_rows`: entries lie within 27 / sqrt(6144) in magnitude.
All inputs are finite; a program needn't handle non-finite values.
Results may differ from a plain program's by a relative error of at most 0.009.
Values may be sent and summed in bfloat16 or wider, within the bound.
A program may use at most 128 MiB of HBM per device.

v0:
```python
import jax
import jax.numpy as jnp
from jax import lax
from jax.sharding import PartitionSpec as P

SEQS = 4
PAIRS = 2
epsilon = 1e-05
dpo_beta = 0.5


def normed_rows(tokens, norm_gain):
    values = tokens.astype(jnp.float32)
    inverse_rms = lax.rsqrt(jnp.mean(values * values, axis=1, keepdims=True) + epsilon)
    return (values * inverse_rms * norm_gain[None, :]).astype(jnp.bfloat16)


def slot_tables(expert_ids, gate_weights, experts, capacity):
    tok_count = expert_ids.shape[0]
    flat_ids = expert_ids.reshape(-1)
    onehot = (flat_ids[:, None] == jnp.arange(experts, dtype=jnp.int32)[None, :]).astype(jnp.int32)
    earlier = jnp.cumsum(onehot, axis=0) - onehot
    position = jnp.sum(earlier * onehot, axis=1)
    slot_index = flat_ids * capacity + position
    slot_match = (
        slot_index[:, None] == jnp.arange(experts * capacity, dtype=jnp.int32)[None, :]
    ).astype(jnp.float32)
    slot_match = slot_match.reshape(tok_count, 2, experts * capacity)
    placement = jnp.sum(slot_match, axis=1)
    mixing = jnp.sum(slot_match * gate_weights[:, :, None], axis=1)
    return (placement, mixing)


def body(
    tokens,
    norm_gain,
    expert_ids,
    gate_weights,
    w_gate,
    w_up,
    w_down,
    label_rows,
    seg_ids,
    pair_slot,
    ref_scores,
):
    group_count = tokens.shape[0]
    experts = lax.axis_size("expert")
    expert_index = lax.axis_index("expert")
    capacity = max(2, 9 * group_count // (4 * experts))
    tensor_count = lax.axis_size("tensor")
    column_width = tokens.shape[1] // tensor_count
    tensor_index = lax.axis_index("tensor")
    own_count = group_count // experts
    normed = normed_rows(tokens, norm_gain)
    placement, mixing = slot_tables(expert_ids, gate_weights, experts, capacity)
    own_place = lax.dynamic_slice_in_dim(placement, expert_index * capacity, capacity, 1)
    own_mixing = lax.dynamic_slice_in_dim(mixing, expert_index * capacity, capacity, 1)
    arrived = jnp.dot(
        own_place.T.astype(jnp.bfloat16), normed, preferred_element_type=jnp.float32
    ).astype(jnp.bfloat16)
    gate_local = w_gate[0]
    up_local = w_up[0]
    down_local = w_down[0]
    own_columns = lax.dynamic_slice_in_dim(arrived, tensor_index * column_width, column_width, 1)
    group_rows = lax.all_gather(own_columns, "dp", axis=0, tiled=True)
    block_cols = lax.all_gather(group_rows, "tensor", axis=1, tiled=True)
    gate_sum = jnp.dot(block_cols, gate_local, preferred_element_type=jnp.float32)
    up_sum = jnp.dot(block_cols, up_local, preferred_element_type=jnp.float32)
    hidden = (jax.nn.silu(gate_sum) * up_sum).astype(jnp.bfloat16)
    hidden_block = lax.all_gather(hidden, "tensor", axis=1, tiled=True)
    own_rows = lax.psum_scatter(
        jnp.dot(hidden_block, down_local, preferred_element_type=jnp.float32).astype(jnp.bfloat16),
        "dp",
        scatter_dimension=0,
        tiled=True,
    )
    weighted = jnp.dot(own_mixing, own_rows.astype(jnp.float32), precision=lax.Precision.HIGHEST)
    expert_mix = lax.psum_scatter(
        weighted.astype(jnp.bfloat16), "expert", scatter_dimension=0, tiled=True
    ).astype(jnp.float32)
    token_rows = lax.dynamic_slice_in_dim(tokens, expert_index * own_count, own_count, 0)
    residual = lax.dynamic_slice_in_dim(
        token_rows, tensor_index * column_width, column_width, 1
    ).astype(jnp.float32)
    mixed = residual + expert_mix
    layer_out = mixed.astype(jnp.bfloat16)
    token_score = jnp.sum(mixed * label_rows.astype(jnp.float32), axis=1)
    sequence_ids = lax.dynamic_slice_in_dim(seg_ids[0], expert_index * own_count, own_count, 0)
    member = (sequence_ids[:, None] == jnp.arange(SEQS, dtype=jnp.int32)[None, :]).astype(
        jnp.float32
    )
    partial_value = jnp.sum(member * token_score[:, None], axis=0)
    totals = lax.psum(partial_value, ("expert", "tensor"))
    slots_here = pair_slot[0]
    polarity = (1 - 2 * (slots_here % 2)).astype(jnp.float32)
    pair_member = (
        (slots_here // 2)[:, None] == jnp.arange(PAIRS, dtype=jnp.int32)[None, :]
    ).astype(jnp.float32)
    margins = dpo_beta * jnp.sum(
        pair_member * (polarity * (totals - ref_scores[0]))[:, None], axis=0
    )
    return (layer_out, margins[None, :])


def solution(mesh):
    placed = (
        P("dp", None),
        P(),
        P("dp", None),
        P("dp", None),
        P("expert", None, ("dp", "tensor")),
        P("expert", None, ("dp", "tensor")),
        P("expert", "dp", "tensor"),
        P(("dp", "expert"), "tensor"),
        P("dp", None),
        P("dp", None),
        P("dp", None),
    )
    return jax.shard_map(
        body,
        mesh=mesh,
        in_specs=placed,
        out_specs=(P(("dp", "expert"), "tensor"), P("dp", None)),
        check_vma=False,
    )
```

profile of v0, /device:TPU:0, one launch (start us, length us, event | category | flops | bytes accessed | tf_op | source)
XLA Modules:
  0.0 209.0 jit_solution(1095833018729671077)
XLA Ops:
  7.2 0.8 copy.31
  8.0 0.1 eq.73
  8.2 0.1 eq.69
  8.3 1.2 reduce-window.6
  9.5 0.1 slice.8
  9.6 0.1 copy.33
  9.8 0.1 copy.34
  9.9 0.1 add_bitcast_fusion
  10.0 0.1 reduce_sum.66
  10.1 0.1 copy.35
  10.2 0.7 multiply_add_fusion
  10.9 1.8 fusion.9
  12.7 0.8 select_reduce_fusion
  13.4 2.1 %fusion.18 = bf16[72,6144]{1,0:T(8,128)(2,1)S(1)} fusion(bf16[128,6144]{1,0:T(8,128)(2,1)} %param.11, f32[6144]{0:T(1024)} %param.12, f32[128]{0:T(128)S(1)} %add_rsqrt_fusion, bf16[128,288]{0,1:T(8,128)(2,1)S(1)} %get-tuple-element.3, s32[]{:T(128)S(6)} %select_n.36), kind=kOutput, calls=%fused_computation.15 | convolution fusion | flops 116391936 | bytes 2501124 | tf_op jit(solution)/shard_map/dot_general | solution.py:59
  15.5 0.8 dynamic-slice_convert_fusion
  16.4 43.1 %all-gather.4.cloned.1.call-done = bf16[288,3072]{1,0:T(8,128)(2,1)} async-done(((bf16[72,3072]{1,0:T(8,128)(2,1)}), bf16[288,3072]{1,0:T(8,128)(2,1)}) %all-gather.4.cloned.1.call-update) | async-done | bytes 1769488 | tf_op jit(solution)/shard_map/all_gather | solution.py:66
  59.6 13.0 %all-gather.6.cloned.1.call-done = bf16[288,6144]{1,0:T(8,128)(2,1)} async-done(((bf16[288,3072]{1,0:T(8,128)(2,1)}), bf16[288,6144]{1,0:T(8,128)(2,1)}) %all-gather.6.cloned.1.call-update) | async-done | bytes 3538960 | tf_op jit(solution)/shard_map/all_gather | solution.py:67
  72.6 13.2 %fusion.4 = f32[288,1536]{1,0:T(8,128)S(1)} fusion(bf16[288,6144]{1,0:T(8,128)(2,1)} %all-gather.6.cloned.1.call-done, bf16[1,6144,1536]{2,1,0:T(8,128)(2,1)} %param.15), kind=kOutput, calls=%fused_computation.4 | convolution fusion | flops 5435817984 | bytes 24182784 | tf_op jit(solution)/shard_map/dot_general | solution.py:68
  85.8 11.0 %fusion.15 = bf16[288,1536]{1,0:T(8,128)(2,1)} fusion(bf16[288,6144]{1,0:T(8,128)(2,1)S(1)} %copy-done.4, bf16[1,6144,1536]{2,1,0:T(8,128)(2,1)} %param.16, f32[288,1536]{1,0:T(8,128)S(1)} %fusion.4), kind=kOutput, calls=%fused_computation.14 | convolution fusion | flops 5438472192 | bytes 25067520 | tf_op jit(solution)/shard_map/dot_general | solution.py:69
  96.8 0.0 reduce-scatter.3.cloned.1.call-start
  96.9 11.4 %all-gather.8.cloned.1.call-done = bf16[288,3072]{1,0:T(8,128)(2,1)} async-done(((bf16[288,1536]{1,0:T(8,128)(2,1)}), bf16[288,3072]{1,0:T(8,128)(2,1)}) %all-gather.8.cloned.1.call-update) | async-done | bytes 1769488 | tf_op jit(solution)/shard_map/all_gather | solution.py:71
  108.3 11.1 %fusion.6 = bf16[288,3072]{1,0:T(8,128)(2,1)} fusion(bf16[288,3072]{1,0:T(8,128)(2,1)} %all-gather.8.cloned.1.call-done, bf16[1,3072,3072]{2,1,0:T(8,128)(2,1)} %param.17), kind=kOutput, calls=%fused_computation.6 | convolution fusion | flops 5436702720 | bytes 22413312 | tf_op jit(solution)/shard_map/dot_general | solution.py:73
  119.4 0.0 reduce-scatter.5.cloned.1.call-start
  119.4 39.8 %reduce-scatter.3.cloned.1.call-done = bf16[72,3072]{1,0:T(8,128)(2,1)} async-done(((bf16[288,3072]{1,0:T(8,128)(2,1)}), bf16[72,3072]{1,0:T(8,128)(2,1)}) %reduce-scatter.3.cloned.1.call-update) | async-done | bytes 442384 | tf_op jit(solution)/shard_map/reduce_scatter | solution.py:72
  159.2 2.7 %convolution_convert_fusion = bf16[128,3072]{1,0:T(8,128)(2,1)} fusion(bf16[72,3072]{1,0:T(8,128)(2,1)} %reduce-scatter.3.cloned.1.call-done, f32[128,288]{0,1:T(8,128)S(1)} %get-tuple-element.2, s32[]{:T(128)S(6)} %select_n.36), kind=kOutput, calls=%fused_computation.9 | convolution fusion | flops 340131840 | bytes 1265668 | tf_op jit(solution)/shard_map/dot_general | solution.py:78
  162.0 0.1 fusion.30
  162.0 25.2 %reduce-scatter.5.cloned.1.call-done = bf16[32,3072]{1,0:T(8,128)(2,1)} async-done(((bf16[128,3072]{1,0:T(8,128)(2,1)}), bf16[32,3072]{1,0:T(8,128)(2,1)}) %reduce-scatter.5.cloned.1.call-update) | async-done | bytes 196624 | tf_op jit(solution)/shard_map/reduce_scatter | solution.py:79
  187.2 2.0 multiply_reduce_fusion
  189.2 0.1 select_reduce_fusion.1
  189.4 12.5 %psum.7 = f32[4]{0:T(128)S(1)} all-reduce(f32[4]{0:T(128)S(1)} %select_reduce_fusion.1), channel_id=1, replica_groups=mesh['dp'=4,'expert'=4,'tensor'=2] {'expert','tensor'}, use_global_device_ids=true, to_apply=%region_10.11 | all-reduce | flops 4 | bytes 32 | tf_op jit(solution)/shard_map/psum | solution.py:94
  201.8 0.1 fusion.27
  201.9 0.5 multiply_bitcast_fusion
  (25 shorter events, 0.3 us)
Async XLA Ops:
  7.2 154.8 %copy-start = (s32[1,128]{1,0:T(1,128)S(1)}, s32[1,128]{1,0:T(1,128)}, u32[]{:S(2)}) copy-start(s32[1,128]{1,0:T(1,128)} %param.19) | copy-start | bytes 1540
  7.2 52.3 %all-gather.4.cloned.1.call-start = ((), (), s32[]{:S(2)}) async-start(), calls=%async_computation.2 | async-start | bytes 2211840 | tf_op jit(solution)/shard_map/all_gather | solution.py:66
  16.4 56.2 %all-gather.6.cloned.1.call-start = ((), (), s32[]{:S(2)}) async-start(), calls=%async_computation.3 | async-start | bytes 5308416 | tf_op jit(solution)/shard_map/all_gather | solution.py:67
  59.5 48.7 %all-gather.8.cloned.1.call-start = ((), (), s32[]{:S(2)}) async-start(), calls=%async_computation.4 | async-start | bytes 2654208 | tf_op jit(solution)/shard_map/all_gather | solution.py:71
  72.6 13.2 %copy-start.4 = (bf16[288,6144]{1,0:T(8,128)(2,1)S(1)}, bf16[288,6144]{1,0:T(8,128)(2,1)}, u32[]{:S(2)}) copy-start(bf16[288,6144]{1,0:T(8,128)(2,1)} %all-gather.6.cloned.1.call-done) | copy-start | bytes 10616836
  96.8 62.4 %reduce-scatter.3.cloned.1.call-start = ((), (), s32[]{:S(2)}) async-start(), calls=%async_computation.5 | async-start | bytes 2211840 | tf_op jit(solution)/shard_map/reduce_scatter | solution.py:72
  119.4 67.9 %copy-start.1 = (bf16[32,3072]{1,0:T(8,128)(2,1)S(1)}, bf16[32,3072]{1,0:T(8,128)(2,1)}, u32[]{:S(2)}) copy-start(bf16[32,3072]{1,0:T(8,128)(2,1)} %param.18) | copy-start | bytes 589828
  119.4 70.0 %copy-start.3 = (s32[1,4]{1,0:T(1,128)S(1)}, s32[1,4]{1,0:T(1,128)}, u32[]{:S(2)}) copy-start(s32[1,4]{1,0:T(1,128)} %param.20) | copy-start | bytes 52
  119.4 82.5 %copy-start.2 = (f32[1,4]{1,0:T(1,128)S(1)}, f32[1,4]{1,0:T(1,128)}, u32[]{:S(2)}) copy-start(f32[1,4]{1,0:T(1,128)} %param.21) | copy-start | bytes 52
  119.4 67.8 %reduce-scatter.5.cloned.1.call-start = ((), (), s32[]{:S(2)}) async-start(), calls=%async_computation.6 | async-start | bytes 983040 | tf_op jit(solution)/shard_map/reduce_scatter | solution.py:79
Sparse Core Ops, SparseCore 0:
  16.5 42.9 all-gather.3
  61.1 11.5 all-gather.5
  97.0 11.2 all-gather.7
  119.5 39.6 reduce-scatter.2
  162.1 25.1 reduce-scatter.4
where the time goes:
time: 209 us
  waiting for transfers between devices  133 us (64%)
  matrix products  40.1 us (19%)
  between operations  13.9 us (7%)
  blocking collectives  12.5 us (6%)
  other arithmetic  7.38 us (4%)
  local copies, waits for them, and re-layouts  2.45 us (1%)
    all_gather x1, waiting for transfers between devices, body(): group_rows = lax.all_gather(own_columns, 'dp', axis=0, tiled=True)  43.1 us
    reduce_scatter x1, waiting for transfers between devices, body(): lax.psum_scatter(jnp.dot(hidden_block, down_local, preferred_element_type...  39.8 us
    reduce_scatter x1, waiting for transfers between devices, body(): lax.psum_scatter(weighted.astype(jnp.bfloat16), 'expert', scatter_dimensi...  25.2 us
    dot_general x1, matrix products, body(): jnp.dot(block_cols, gate_local, preferred_element_type=jnp.float32)  13.2 us
    all_gather x1, waiting for transfers between devices, body(): block_cols = lax.all_gather(group_rows, 'tensor', axis=1, tiled=True)  13 us
    psum x1, blocking collectives, body(): totals = lax.psum(partial_value, ('expert', 'tensor'))  12.5 us
    all_gather x1, waiting for transfers between devices, body(): hidden_block = lax.all_gather(hidden, 'tensor', axis=1, tiled=True)  11.4 us
    dot_general x1, matrix products, body(): jnp.dot(hidden_block, down_local, preferred_element_type=jnp.float32)  11.1 us
  transfers between devices with their start and end apart: 5, of which 5 were waited for; matrix products, arithmetic and copies ran while one was open for 0% of the time, Pallas kernels for 0%

commit v1 on v0

--- a/solution.py
+++ b/solution.py
@@ -63,7 +63,12 @@
     up_local = w_up[0]
     down_local = w_down[0]
     own_columns = lax.dynamic_slice_in_dim(arrived, tensor_index * column_width, column_width, 1)
-    group_rows = lax.all_gather(own_columns, "dp", axis=0, tiled=True)
+    ring = [own_columns]
+    for hop in range(3):
+        ring.append(lax.ppermute(ring[-1], "dp", [(dev, (dev + 1) % 4) for dev in range(4)]))
+    group_rows = jnp.roll(
+        jnp.concatenate(ring[::-1], axis=0), (lax.axis_index("dp") + 1) * ring[0].shape[0], axis=0
+    )
     block_cols = lax.all_gather(group_rows, "tensor", axis=1, tiled=True)
     gate_sum = jnp.dot(block_cols, gate_local, preferred_element_type=jnp.float32)
     up_sum = jnp.dot(block_cols, up_local, preferred_element_type=jnp.float32)

time: 209 us -> 206 us (0.986)
  waiting for transfers between devices: 133 us -> 125 us
  starting transfers between devices: 0.2 us -> 3.27 us
    all_gather x1 -> x0, waiting for transfers between devices: 43.1 us -> none  [body(): group_rows = lax.all_gather(own_columns, 'dp', axis=0, tiled=True)]
    ppermute x0 -> x3, waiting for transfers between devices: none -> 37.6 us  [body(): lax.ppermute(ring[-1], 'dp', [(dev, (dev + 1) % 4) for dev in range(4)])]
    ppermute x0 -> x3, starting transfers between devices: none -> 3.11 us  [body(): lax.ppermute(ring[-1], 'dp', [(dev, (dev + 1) % 4) for dev in range(4)])]
    all_gather x1, waiting for transfers between devices: 13 us -> 10.6 us  [body(): block_cols = lax.all_gather(group_rows, 'tensor', axis=1, tiled=True)]
  transfers between devices with their start and end apart: 5 -> 7, of which waited for: 5 -> 7; matrix products, arithmetic and copies ran while one was open for 0% -> 0% of each run, Pallas kernels for 0% -> 0%
where the time goes in v1:
time: 206 us; the launch traced here: 205 us
  waiting for transfers between devices  125 us (61%)
  matrix products  40.1 us (19%)
  between operations  13.9 us (7%)
  blocking collectives  12.5 us (6%)
  other arithmetic  7.38 us (4%)
  local copies, waits for them, and re-layouts  3.61 us (2%)
  starting transfers between devices  3.27 us (2%)
    reduce_scatter x1, waiting for transfers between devices, body(): lax.psum_scatter(jnp.dot(hidden_block, down_local, preferred_element_type...  39.8 us
    ppermute x3, waiting for transfers between devices, body(): lax.ppermute(ring[-1], 'dp', [(dev, (dev + 1) % 4) for dev in range(4)])  37.6 us
    reduce_scatter x1, waiting for transfers between devices, body(): lax.psum_scatter(weighted.astype(jnp.bfloat16), 'expert', scatter_dimensi...  25.2 us
    dot_general x1, matrix products, body(): jnp.dot(block_cols, gate_local, preferred_element_type=jnp.float32)  13.2 us
    psum x1, blocking collectives, body(): totals = lax.psum(partial_value, ('expert', 'tensor'))  12.5 us
    all_gather x1, waiting for transfers between devices, body(): hidden_block = lax.all_gather(hidden, 'tensor', axis=1, tiled=True)  11.3 us
    dot_general x1, matrix products, body(): jnp.dot(hidden_block, down_local, preferred_element_type=jnp.float32)  11.1 us
    dot_general x1, matrix products, body(): up_sum = jnp.dot(block_cols, up_local, preferred_element_type=jnp.float32)  11 us
  transfers between devices with their start and end apart: 7, of which 7 were waited for; matrix products, arithmetic and copies ran while one was open for 0% of the time, Pallas kernels for 0%

profile of v1, /device:TPU:0, one launch (start us, length us, event | category | flops | bytes accessed | tf_op | source)
XLA Modules:
  0.0 205.3 jit_solution(9844908278757200093)
XLA Ops:
  7.2 0.8 copy.31
  8.0 0.1 eq.76
  8.2 0.1 eq.72
  8.3 1.2 reduce-window.6
  9.5 0.1 slice.8
  9.6 0.1 copy.33
  9.8 0.1 copy.34
  9.9 0.1 add_bitcast_fusion
  10.0 0.1 reduce_sum.66
  10.2 0.7 multiply_add_fusion
  10.9 1.8 fusion.9
  12.7 0.8 select_reduce_fusion
  13.4 2.1 %fusion.18 = bf16[72,6144]{1,0:T(8,128)(2,1)S(1)} fusion(bf16[128,6144]{1,0:T(8,128)(2,1)} %param.11, f32[6144]{0:T(1024)} %param.12, f32[128]{0:T(128)S(1)} %add_rsqrt_fusion, bf16[128,288]{0,1:T(8,128)(2,1)S(1)} %get-tuple-element.3, s32[]{:T(128)S(6)} %select_n.48), kind=kOutput, calls=%fused_computation.15 | convolution fusion | flops 116391936 | bytes 2501124 | tf_op jit(solution)/shard_map/dot_general | solution.py:59
  15.6 3.1 %collective-permute-start = (bf16[72,3072]{1,0:T(8,128)(2,1)S(1)}, bf16[72,3072]{1,0:T(8,128)(2,1)S(1)}, u32[]{:S(2)}, u32[]{:S(2)}) collective-permute-start(bf16[72,3072]{1,0:T(8,128)(2,1)S(1)} %dynamic-slice_convert_fusion), channel_id=1, source_target_pairs={{0,8},{8,16},{16,24},{24,0},{1,9},{9,17},{17,25},{25,1},{2,10},{10... | collective-permute-start | bytes 1327112 | tf_op jit(solution)/shard_map/ppermute | solution.py:68
  18.7 12.2 %collective-permute-done = bf16[72,3072]{1,0:T(8,128)(2,1)S(1)} collective-permute-done((bf16[72,3072]{1,0:T(8,128)(2,1)S(1)}, bf16[72,3072]{1,0:T(8,128)(2,1)S(1)}, u32[]{:S(2)}, u32[]{:S(2)}) %collective-permute-start) | collective-permute-done | bytes 442400 | tf_op jit(solution)/shard_map/ppermute | solution.py:68
  30.9 13.1 %collective-permute-done.1 = bf16[72,3072]{1,0:T(8,128)(2,1)S(1)} collective-permute-done((bf16[72,3072]{1,0:T(8,128)(2,1)S(1)}, bf16[72,3072]{1,0:T(8,128)(2,1)S(1)}, u32[]{:S(2)}, u32[]{:S(2)}) %collective-permute-start.1) | collective-permute-done | bytes 442400 | tf_op jit(solution)/shard_map/ppermute | solution.py:68
  44.0 12.3 %collective-permute-done.2 = bf16[72,3072]{1,0:T(8,128)(2,1)S(1)} collective-permute-done((bf16[72,3072]{1,0:T(8,128)(2,1)S(1)}, bf16[72,3072]{1,0:T(8,128)(2,1)S(1)}, u32[]{:S(2)}, u32[]{:S(2)}) %collective-permute-start.2) | collective-permute-done | bytes 442400 | tf_op jit(solution)/shard_map/ppermute | solution.py:68
  56.6 1.7 constant_dynamic-slice_fusion
  58.4 10.6 %all-gather.3.cloned.1.call-done = bf16[288,6144]{1,0:T(8,128)(2,1)} async-done(((bf16[288,3072]{1,0:T(8,128)(2,1)}), bf16[288,6144]{1,0:T(8,128)(2,1)}) %all-gather.3.cloned.1.call-update) | async-done | bytes 3538960 | tf_op jit(solution)/shard_map/all_gather | solution.py:72
  68.9 13.2 %fusion.4 = f32[288,1536]{1,0:T(8,128)S(1)} fusion(bf16[288,6144]{1,0:T(8,128)(2,1)} %all-gather.3.cloned.1.call-done, bf16[1,6144,1536]{2,1,0:T(8,128)(2,1)} %param.15), kind=kOutput, calls=%fused_computation.4 | convolution fusion | flops 5435817984 | bytes 24182784 | tf_op jit(solution)/shard_map/dot_general | solution.py:73
  82.1 11.0 %fusion.15 = bf16[288,1536]{1,0:T(8,128)(2,1)} fusion(bf16[288,6144]{1,0:T(8,128)(2,1)S(1)} %copy-done.4, bf16[1,6144,1536]{2,1,0:T(8,128)(2,1)} %param.16, f32[288,1536]{1,0:T(8,128)S(1)} %fusion.4), kind=kOutput, calls=%fused_computation.14 | convolution fusion | flops 5438472192 | bytes 25067520 | tf_op jit(solution)/shard_map/dot_general | solution.py:74
  93.2 11.3 %all-gather.5.cloned.1.call-done = bf16[288,3072]{1,0:T(8,128)(2,1)} async-done(((bf16[288,1536]{1,0:T(8,128)(2,1)}), bf16[288,3072]{1,0:T(8,128)(2,1)}) %all-gather.5.cloned.1.call-update) | async-done | bytes 1769488 | tf_op jit(solution)/shard_map/all_gather | solution.py:76
  104.6 11.1 %fusion.6 = bf16[288,3072]{1,0:T(8,128)(2,1)} fusion(bf16[288,3072]{1,0:T(8,128)(2,1)} %all-gather.5.cloned.1.call-done, bf16[1,3072,3072]{2,1,0:T(8,128)(2,1)} %param.17), kind=kOutput, calls=%fused_computation.6 | convolution fusion | flops 5436702720 | bytes 22413312 | tf_op jit(solution)/shard_map/dot_general | solution.py:78
  115.7 39.8 %reduce-scatter.3.cloned.1.call-done = bf16[72,3072]{1,0:T(8,128)(2,1)} async-done(((bf16[288,3072]{1,0:T(8,128)(2,1)}), bf16[72,3072]{1,0:T(8,128)(2,1)}) %reduce-scatter.3.cloned.1.call-update) | async-done | bytes 442384 | tf_op jit(solution)/shard_map/reduce_scatter | solution.py:77
  155.5 2.7 %convolution_convert_fusion = bf16[128,3072]{1,0:T(8,128)(2,1)} fusion(bf16[72,3072]{1,0:T(8,128)(2,1)} %reduce-scatter.3.cloned.1.call-done, f32[128,288]{0,1:T(8,128)S(1)} %get-tuple-element.2, s32[]{:T(128)S(6)} %select_n.48), kind=kOutput, calls=%fused_computation.9 | convolution fusion | flops 340131840 | bytes 1265668 | tf_op jit(solution)/shard_map/dot_general | solution.py:83
  158.3 0.1 fusion.30
  158.3 25.2 %reduce-scatter.5.cloned.1.call-done = bf16[32,3072]{1,0:T(8,128)(2,1)} async-done(((bf16[128,3072]{1,0:T(8,128)(2,1)}), bf16[32,3072]{1,0:T(8,128)(2,1)}) %reduce-scatter.5.cloned.1.call-update) | async-done | bytes 196624 | tf_op jit(solution)/shard_map/reduce_scatter | solution.py:84
  183.5 2.0 multiply_reduce_fusion
  185.5 0.1 select_reduce_fusion.1
  185.7 12.5 %psum.7 = f32[4]{0:T(128)S(1)} all-reduce(f32[4]{0:T(128)S(1)} %select_reduce_fusion.1), channel_id=1, replica_groups=mesh['dp'=4,'expert'=4,'tensor'=2] {'expert','tensor'}, use_global_device_ids=true, to_apply=%region_10.11 | all-reduce | flops 4 | bytes 32 | tf_op jit(solution)/shard_map/psum | solution.py:99
  198.1 0.1 fusion.29
  198.3 0.5 multiply_bitcast_fusion
  (37 shorter events, 0.7 us)
Async XLA Ops:
  7.2 151.1 %copy-start = (s32[1,128]{1,0:T(1,128)S(1)}, s32[1,128]{1,0:T(1,128)}, u32[]{:S(2)}) copy-start(s32[1,128]{1,0:T(1,128)} %param.19) | copy-start | bytes 1540
  7.2 61.8 %all-gather.3.cloned.1.call-start = ((), (), s32[]{:S(2)}) async-start(), calls=%async_computation.2 | async-start | bytes 5308416 | tf_op jit(solution)/shard_map/all_gather | solution.py:72
  15.6 15.3 %collective-permute-start = (bf16[72,3072]{1,0:T(8,128)(2,1)S(1)}, bf16[72,3072]{1,0:T(8,128)(2,1)S(1)}, u32[]{:S(2)}, u32[]{:S(2)}) collective-permute-start(bf16[72,3072]{1,0:T(8,128)(2,1)S(1)} %dynamic-slice_convert_fusion), channel_id=1, source_target_pairs={{0,8},{8,16},{16,24},{24,0},{1,9},{9,17},{17,25},{25,1},{2,10},{10... | collective-permute-start | bytes 1327112 | tf_op jit(solution)/shard_map/ppermute | solution.py:68
  30.9 13.1 %collective-permute-start.1 = (bf16[72,3072]{1,0:T(8,128)(2,1)S(1)}, bf16[72,3072]{1,0:T(8,128)(2,1)S(1)}, u32[]{:S(2)}, u32[]{:S(2)}) collective-permute-start(bf16[72,3072]{1,0:T(8,128)(2,1)S(1)} %collective-permute-done), channel_id=1, source_target_pairs={{0,8},{8,16},{16,24},{24,0},{1,9},{9,17},{17,25},{25,1},{2,10},{10... | collective-permute-start | bytes 1327112 | tf_op jit(solution)/shard_map/ppermute | solution.py:68
  44.0 12.3 %collective-permute-start.2 = (bf16[72,3072]{1,0:T(8,128)(2,1)S(1)}, bf16[72,3072]{1,0:T(8,128)(2,1)S(1)}, u32[]{:S(2)}, u32[]{:S(2)}) collective-permute-start(bf16[72,3072]{1,0:T(8,128)(2,1)S(1)} %collective-permute-done.1), channel_id=1, source_target_pairs={{0,8},{8,16},{16,24},{24,0},{1,9},{9,17},{17,25},{25,1},{2,10},{10... | collective-permute-start | bytes 1327112 | tf_op jit(solution)/shard_map/ppermute | solution.py:68
  58.3 46.3 %all-gather.5.cloned.1.call-start = ((), (), s32[]{:S(2)}) async-start(), calls=%async_computation.3 | async-start | bytes 2654208 | tf_op jit(solution)/shard_map/all_gather | solution.py:76
  68.9 13.2 %copy-start.4 = (bf16[288,6144]{1,0:T(8,128)(2,1)S(1)}, bf16[288,6144]{1,0:T(8,128)(2,1)}, u32[]{:S(2)}) copy-start(bf16[288,6144]{1,0:T(8,128)(2,1)} %all-gather.3.cloned.1.call-done) | copy-start | bytes 10616836
  93.2 62.3 %reduce-scatter.3.cloned.1.call-start = ((), (), s32[]{:S(2)}) async-start(), calls=%async_computation.4 | async-start | bytes 2211840 | tf_op jit(solution)/shard_map/reduce_scatter | solution.py:77
  115.7 67.9 %copy-start.1 = (bf16[32,3072]{1,0:T(8,128)(2,1)S(1)}, bf16[32,3072]{1,0:T(8,128)(2,1)}, u32[]{:S(2)}) copy-start(bf16[32,3072]{1,0:T(8,128)(2,1)} %param.18) | copy-start | bytes 589828
  115.7 70.0 %copy-start.3 = (s32[1,4]{1,0:T(1,128)S(1)}, s32[1,4]{1,0:T(1,128)}, u32[]{:S(2)}) copy-start(s32[1,4]{1,0:T(1,128)} %param.20) | copy-start | bytes 52
  115.7 82.5 %copy-start.2 = (f32[1,4]{1,0:T(1,128)S(1)}, f32[1,4]{1,0:T(1,128)}, u32[]{:S(2)}) copy-start(f32[1,4]{1,0:T(1,128)} %param.21) | copy-start | bytes 52
  115.7 67.8 %reduce-scatter.5.cloned.1.call-start = ((), (), s32[]{:S(2)}) async-start(), calls=%async_computation.5 | async-start | bytes 983040 | tf_op jit(solution)/shard_map/reduce_scatter | solution.py:84
Sparse Core Ops, SparseCore 0:
  58.4 10.4 all-gather.2
  93.3 11.2 all-gather.4
  115.8 39.6 reduce-scatter.2
  158.4 25.1 reduce-scatter.4
